TPU v7x, 512 devices: a whole 4x8x8 slice. The times are simulated.
512 devices in a mesh: dp: 32 (over x, z), tp: 16 (over y, core).
Axes of the slice: x: 4, y: 8, z: 8, core: 2. Of those that a mesh axis runs over, the one named last changes fastest.
Arguments:
- queries: bfloat16 [1024, 128, 576], P(('dp', 'tp')), may hold values from -40 to 40
- latent_cache: bfloat16 [1024, 256, 576], P(('dp', 'tp')), may hold values from -5 to 5
- lengths: int32 [1024], P(('dp', 'tp')), may hold values from 1 to 256, 65536 in all
- value_weight: bfloat16 [128, 512, 128], P('tp'), may hold values from -0.25 to 0.25
- output_weight: bfloat16 [16384, 7168], P('tp', 'dp'), may hold values from -0.046875 to 0.046875
Outputs:
- attended: bfloat16 [1024, 7168], P(('dp', 'tp'))
All inputs are finite; a program needn't handle non-finite values. No bound on the sum of `lengths` on one device may be relied on, other than what follows from the above.
Results may differ from a plain program's by a relative error of at most 0.0065.
Values may be sent and summed in bfloat16 or wider, within the bound.
No kernel may reach another device: no remote copies, remote signals or barrier semaphores. Data moves between devices by JAX's collectives and lax.ppermute only.
A program may use at most 64 MiB of HBM per device.

v0:
```python
import jax
import jax.numpy as jnp
from jax import lax
from jax.sharding import PartitionSpec as P

score_scale = 192.0 ** (-0.5)


def local(queries, latent_cache, lengths, value_weight, output_weight):
    requests = queries.shape[0]
    groups = lax.axis_size("tp")
    columns = lax.axis_size("dp")
    latent_width = value_weight.shape[1]
    scores = (
        jnp.einsum("rhe,rje->rhj", queries, latent_cache, preferred_element_type=jnp.float32)
        * score_scale
    )
    alive_mask = lax.broadcasted_iota(jnp.int32, scores.shape, 2) < lengths[:, None, None]
    scores = jnp.where(alive_mask, scores, -1e30)
    row_max = jnp.max(scores, axis=2, keepdims=True)
    powers = jnp.exp(scores - row_max)
    weights = (powers / jnp.sum(powers, axis=2, keepdims=True)).astype(jnp.bfloat16)
    mixture = jnp.einsum("rhj,rje->rhe", weights, latent_cache, preferred_element_type=jnp.float32)
    latent = mixture[:, :, :latent_width].astype(jnp.bfloat16)
    swapped = lax.all_to_all(latent, "tp", split_axis=1, concat_axis=0, tiled=True)
    values = jnp.einsum("qhd,hde->qhe", swapped, value_weight, preferred_element_type=jnp.float32)
    values = values.astype(jnp.bfloat16).reshape(groups, requests, -1)
    everyone = lax.all_gather(values, "dp", axis=1, tiled=True)
    all_values = everyone.reshape(groups * columns * requests, -1)
    summed = lax.psum_scatter(
        jnp.dot(all_values, output_weight, preferred_element_type=jnp.float32),
        "tp",
        scatter_dimension=0,
        tiled=True,
    )
    rounded = summed.astype(jnp.bfloat16)
    return lax.all_to_all(rounded, "dp", split_axis=0, concat_axis=1, tiled=True)


def solution(mesh):
    return jax.shard_map(
        local,
        mesh=mesh,
        in_specs=(
            P(("dp", "tp"), None, None),
            P(("dp", "tp"), None, None),
            P(("dp", "tp")),
            P("tp", None, None),
            P("tp", "dp"),
        ),
        out_specs=P(("dp", "tp"), None),
        check_vma=False,
    )
```

profile of v0, /device:TPU:2, one launch (start us, length us, event | category | flops | bytes accessed | tf_op | source)
XLA Modules:
  0.0 203.4 jit_solution(8184634764328297941)
XLA Ops:
  6.5 0.0 copy-start
  6.5 0.0 all-gather.2.cloned.1.call-start
  6.5 1.5 fusion.3
  8.1 0.2 fusion.8
  8.3 1.6 fusion.5
  9.9 0.3 copy.16
  10.2 18.2 %all_to_all.37 = bf16[2,128,512]{2,0,1:T(2,128)(2,1)S(1)} all-to-all(bf16[2,128,512]{2,0,1:T(2,128)(2,1)S(1)} %copy.16), channel_id=1, replica_groups=mesh['dp'=32,'tp'=16] {'tp'}, dimensions={1} | all-to-all | bytes 524288 | tf_op jit(solution)/shard_map/all_to_all | solution.py:25
  28.4 0.2 copy.23
  28.6 0.1 all_to_all.30
  28.7 0.0 copy-done
  28.7 0.3 fusion.4
  29.0 0.6 copy.19
  29.7 0.0 all-gather.2.cloned.1.call-update
  29.7 0.0 copy-start.1
  29.7 0.0 reduce-scatter.2.cloned.1.call-start
  29.7 83.9 %all-gather.2.cloned.1.call-done = bf16[16,64,1024]{2,0,1:T(8,128)(2,1)} async-done(((bf16[16,2,1024]{2,0,1:T(8,128)(2,1)}), bf16[16,64,1024]{2,0,1:T(8,128)(2,1)}) %all-gather.2.cloned.1.call-update) | async-done | bytes 2097168 | tf_op jit(solution)/shard_map/all_gather | solution.py:28
  113.6 2.7 %copy.20 = bf16[16,64,1024]{2,1,0:T(8,128)(2,1)S(1)} copy(bf16[16,64,1024]{2,0,1:T(8,128)(2,1)} %all-gather.2.cloned.1.call-done) | data formatting | bytes 4194304 | tf_op jit(solution)/shard_map/all_gather | solution.py:28
  116.4 0.0 copy-done.1
  116.4 1.7 fusion.9
  118.1 0.0 reduce-scatter.2.cloned.1.call-update
  118.2 57.8 %reduce-scatter.2.cloned.1.call-done = f32[64,224]{1,0:T(8,128)} async-done(((f32[1024,224]{1,0:T(8,128)}), f32[64,224]{1,0:T(8,128)}) %reduce-scatter.2.cloned.1.call-update) | async-done | bytes 57360 | tf_op jit(solution)/shard_map/reduce_scatter | solution.py:30
  175.9 0.8 convert_element_type.16
  176.8 19.0 %all_to_all.38 = bf16[32,2,224]{2,1,0:T(2,128)(2,1)S(1)} all-to-all(bf16[32,2,224]{2,1,0:T(2,128)(2,1)S(1)} %all_to_all.31), channel_id=1, replica_groups=mesh['dp'=32,'tp'=16] {'dp'}, dimensions={0} | all-to-all | bytes 57344 | tf_op jit(solution)/shard_map/all_to_all | solution.py:37
  195.8 0.7 all_to_all.34
  (5 shorter events, 0.1 us)
Async XLA Ops:
  6.5 22.1 %copy-start = (bf16[8,512,128]{2,1,0:T(8,128)(2,1)S(1)}, bf16[8,512,128]{2,1,0:T(8,128)(2,1)}, u32[]{:S(2)}) copy-start(bf16[8,512,128]{2,1,0:T(8,128)(2,1)} %param.8) | copy-start | bytes 3145732
  6.5 107.1 %all-gather.2.cloned.1.call-start = ((), (), s32[]{:S(2)}) async-start(), calls=%async_computation.3 | async-start | bytes 2162688 | tf_op jit(solution)/shard_map/all_gather | solution.py:28
  29.7 86.7 %copy-start.1 = (bf16[1024,224]{0,1:T(8,128)(2,1)S(1)}, bf16[1024,224]{0,1:T(8,128)(2,1)}, u32[]{:S(2)}) copy-start(bf16[1024,224]{0,1:T(8,128)(2,1)} %param.9) | copy-start | bytes 1376260
  29.7 146.2 %reduce-scatter.2.cloned.1.call-start = ((), (), s32[]{:S(2)}) async-start(), calls=%async_computation.4 | async-start | bytes 1114112 | tf_op jit(solution)/shard_map/reduce_scatter | solution.py:30
Sparse Core Ops, SparseCore 0:
  29.8 83.7 all-gather.1
  118.3 57.6 reduce-scatter.1
where the time goes:
time: 204 us; the launch traced here: 203 us
  waiting for transfers between devices  142 us (70%)
  blocking collectives  37.2 us (18%)
  between operations  13.5 us (7%)
  matrix products  5.14 us (3%)
  local copies, waits for them, and re-layouts  4.78 us (2%)
    all_gather x1, waiting for transfers between devices, local(): everyone = lax.all_gather(values, 'dp', axis=1, tiled=True)  83.9 us
    reduce_scatter x1, waiting for transfers between devices, local(): lax.psum_scatter(jnp.dot(all_values, output_weight, preferred_element_typ...  57.8 us
    all_to_all x1, blocking collectives, local(): lax.all_to_all(rounded, 'dp', split_axis=0, concat_axis=1, tiled=True)  19 us
    all_to_all x1, blocking collectives, local(): lax.all_to_all(latent, 'tp', split_axis=1, concat_axis=0, tiled=True)  18.2 us
  transfers between devices with their start and end apart: 2, of which 2 were waited for; matrix products, arithmetic and copies ran while one was open for 0% of the time, Pallas kernels for 0%

commit v1 on v0

--- a/solution.py
+++ b/solution.py
@@ -25,7 +25,9 @@
     swapped = lax.all_to_all(latent, "tp", split_axis=1, concat_axis=0, tiled=True)
     values = jnp.einsum("qhd,hde->qhe", swapped, value_weight, preferred_element_type=jnp.float32)
     values = values.astype(jnp.bfloat16).reshape(groups, requests, -1)
-    everyone = lax.all_gather(values, "dp", axis=1, tiled=True)
+    everyone = jnp.concatenate(
+        lax.all_to_all(jnp.stack([values] * lax.axis_size("dp")), "dp", 0, 0), axis=1
+    )
     all_values = everyone.reshape(groups * columns * requests, -1)
     summed = lax.psum_scatter(
         jnp.dot(all_values, output_weight, preferred_element_type=jnp.float32),

time: 204 us -> 185 us (0.907)
  waiting for transfers between devices: 142 us -> 54.4 us
  blocking collectives: 37.2 us -> 99.7 us
  local copies, waits for them, and re-layouts: 4.78 us -> 9.4 us
    all_gather x1 -> x0, waiting for transfers between devices: 83.9 us -> none  [local(): everyone = lax.all_gather(values, 'dp', axis=1, tiled=True)]
    all_to_all x0 -> x1, blocking collectives: none -> 62.7 us  [local(): lax.all_to_all(jnp.stack([values] * lax.axis_size('dp')), 'dp', 0, 0)]
    another operation x0 -> x3, local copies, waits for them, and re-layouts: none -> 4.65 us  [the longest x1 2.75 us: local(): all_values = everyone.reshape(groups * columns * requests, -1)]
    reduce_scatter x1, waiting for transfers between devices: 57.8 us -> 54.3 us  [local(): lax.psum_scatter(jnp.dot(all_values, output_weight, preferred_element_typ...]
    all_gather x1 -> x0, local copies, waits for them, and re-layouts: 2.74 us -> none  [local(): everyone = lax.all_gather(values, 'dp', axis=1, tiled=True)]
    reshape x2 -> x1, local copies, waits for them, and re-layouts: 0.66 us -> 3.37 us  [local(): jnp.concatenate(lax.all_to_all(jnp.stack([values] * lax.axis_size('dp')),...]
  transfers between devices with their start and end apart: 2 -> 1, of which waited for: 2 -> 1; matrix products, arithmetic and copies ran while one was open for 0% -> 0% of each run, Pallas kernels for 0% -> 0%
where the time goes in v1:
time: 185 us; the launch traced here: 184 us
  blocking collectives  99.7 us (54%)
  waiting for transfers between devices  54.4 us (29%)
  between operations  13.5 us (7%)
  local copies, waits for them, and re-layouts  9.4 us (5%)
  matrix products  6.16 us (3%)
    all_to_all x1, blocking collectives, local(): lax.all_to_all(jnp.stack([values] * lax.axis_size('dp')), 'dp', 0, 0)  62.7 us
    reduce_scatter x1, waiting for transfers between devices, local(): lax.psum_scatter(jnp.dot(all_values, output_weight, preferred_element_typ...  54.3 us
    all_to_all x1, blocking collectives, local(): lax.all_to_all(rounded, 'dp', split_axis=0, concat_axis=1, tiled=True)  18.8 us
    all_to_all x1, blocking collectives, local(): lax.all_to_all(latent, 'tp', split_axis=1, concat_axis=0, tiled=True)  18.2 us
  transfers between devices with their start and end apart: 1, of which 1 were waited for; matrix products, arithmetic and copies ran while one was open for 0% of the time, Pallas kernels for 0%

profile of v1, /device:TPU:2, one launch (start us, length us, event | category | flops | bytes accessed | tf_op | source)
XLA Modules:
  0.0 184.1 jit_solution(16310146627851482384)
XLA Ops:
  6.5 0.0 copy-start
  6.5 0.0 reduce-scatter.2.cloned.1.call-start
  6.5 1.5 fusion.3
  8.1 0.2 fusion.8
  8.3 1.6 fusion.5
  9.9 0.3 copy.11
  10.2 18.2 %all_to_all.42 = bf16[2,128,512]{2,0,1:T(2,128)(2,1)S(1)} all-to-all(bf16[2,128,512]{2,0,1:T(2,128)(2,1)S(1)} %copy.11), channel_id=1, replica_groups=mesh['dp'=32,'tp'=16] {'tp'}, dimensions={1} | all-to-all | bytes 524288 | tf_op jit(solution)/shard_map/all_to_all | solution.py:25
  28.4 0.2 copy.17
  28.6 0.1 all_to_all.33
  28.7 0.0 copy-done
  28.7 0.3 fusion.4
  29.0 1.9 %stack.3 = bf16[32,16,2,1024]{3,2,1,0:T(2,128)(2,1)S(1)} broadcast(bf16[16,2,1024]{2,1,0:T(2,128)(2,1)S(1)} %stack_reshape.2), dimensions={1,2,3} | broadcast | bytes 2162688 | tf_op jit(solution)/shard_map/stack | solution.py:29
  30.9 62.7 %all_to_all.43 = bf16[32,16,2,1024]{3,2,1,0:T(2,128)(2,1)S(1)} all-to-all(bf16[32,16,2,1024]{3,2,1,0:T(2,128)(2,1)S(1)} %stack.3), channel_id=1, replica_groups=mesh['dp'=32,'tp'=16] {'dp'}, dimensions={0} | all-to-all | bytes 4194304 | tf_op jit(solution)/shard_map/all_to_all | solution.py:29
  93.6 3.4 %copy.14 = bf16[16,32,2,1024]{3,2,1,0:T(2,128)(2,1)} copy(bf16[16,32,2,1024]{3,2,0,1:T(2,128)(2,1)S(1)} %bitcast.19) | data formatting | bytes 4194304 | tf_op jit(solution)/shard_map/reshape | solution.py:28
  97.0 2.7 %reshape_reshape.3 = bf16[1024,1024]{1,0:T(8,128)(2,1)S(1)} reshape(bf16[16,32,2,1024]{3,2,1,0:T(2,128)(2,1)} %copy.14) | data formatting | bytes 4194304 | tf_op jit(solution)/shard_map/reshape;reshape | solution.py:31
  99.7 2.7 %fusion.9 = f32[1024,224]{1,0:T(8,128)} fusion(bf16[1024,1024]{1,0:T(8,128)(2,1)S(1)} %reshape_reshape.3, bf16[1024,224]{0,1:T(8,128)(2,1)} %param.9), kind=kOutput, calls=%fused_computation.15 | convolution fusion | flops 469762048 | bytes 3473408 | tf_op jit(solution)/shard_map/dot_general | solution.py:33
  102.5 0.0 reduce-scatter.2.cloned.1.call-update
  102.5 54.3 %reduce-scatter.2.cloned.1.call-done = f32[64,224]{1,0:T(8,128)} async-done(((f32[1024,224]{1,0:T(8,128)}), f32[64,224]{1,0:T(8,128)}) %reduce-scatter.2.cloned.1.call-update) | async-done | bytes 57360 | tf_op jit(solution)/shard_map/reduce_scatter | solution.py:32
  156.9 0.8 convert_element_type.16
  157.7 18.8 %all_to_all.44 = bf16[32,2,224]{2,1,0:T(2,128)(2,1)S(1)} all-to-all(bf16[32,2,224]{2,1,0:T(2,128)(2,1)S(1)} %all_to_all.35), channel_id=1, replica_groups=mesh['dp'=32,'tp'=16] {'dp'}, dimensions={0} | all-to-all | bytes 57344 | tf_op jit(solution)/shard_map/all_to_all | solution.py:39
  176.5 0.7 all_to_all.38
  (5 shorter events, 0.1 us)
Async XLA Ops:
  6.5 22.1 %copy-start = (bf16[8,512,128]{2,1,0:T(8,128)(2,1)S(1)}, bf16[8,512,128]{2,1,0:T(8,128)(2,1)}, u32[]{:S(2)}) copy-start(bf16[8,512,128]{2,1,0:T(8,128)(2,1)} %param.8) | copy-start | bytes 3145732
  6.5 150.3 %reduce-scatter.2.cloned.1.call-start = ((), (), s32[]{:S(2)}) async-start(), calls=%async_computation.4 | async-start | bytes 1114112 | tf_op jit(solution)/shard_map/reduce_scatter | solution.py:32
Sparse Core Ops, SparseCore 0:
  102.6 54.1 reduce-scatter.1
